TPU v7x, 32 devices: a whole 2x2x4 slice. The times are simulated.
32 devices in a mesh: req: 16 (over z, x, core), head: 2 (over y).
Axes of the slice: x: 2, y: 2, z: 4, core: 2. Of those that a mesh axis runs over, the one named last changes fastest.
Arguments:
- draft_ids: int32 [256, 16], P('req'), may hold values from 0 to 63999
- worker_slot: int32 [256], P('req'), may hold values from 0 to 255, as said below
- accepted: int32 [256], P('req'), may hold values from 0 to 16
- embedding: bfloat16 [64000, 2048], P('req', 'head'), may hold values from -120 to 120
- w_query: bfloat16 [2048, 2048], P('req', 'head'), may hold values from -0.125 to 0.125
- w_key: bfloat16 [2048, 2048], P('req', 'head'), may hold values from -0.125 to 0.125
- w_value: bfloat16 [2048, 4096], P('req', 'head'), may hold values from -0.125 to 0.125
- w_gate: bfloat16 [2048, 4096], P('req', 'head'), may hold values from -0.125 to 0.125
- old_state: bfloat16 [256, 8, 256, 512], P('req', 'head'), may hold values from -4 to 4
Outputs:
- hidden: bfloat16 [256, 16, 4096], P('req', None, 'head')
- new_state: bfloat16 [256, 8, 256, 512], P('req', 'head')
Inputs may be any that keep to these rules, and one draw needn't show every extreme that they name: worker_slot is a permutation of 0 to 255; request r is handled by worker worker_slot[r] // 16 at position worker_slot[r] % 16; the 16 requests of one owner (aligned blocks of 16) go to 16 different workers.
All inputs are finite; a program needn't handle non-finite values.
Results may differ from a plain program's by a relative error of at most 0.0095.
Values may be sent and summed in bfloat16 or wider, within the bound.
No kernel may reach another device: no remote copies, remote signals or barrier semaphores. Data moves between devices by JAX's collectives and lax.ppermute only.
A program may use at most 192 MiB of HBM per device.

v0:
```python
import jax
import jax.numpy as jnp
from jax import lax
from jax.sharding import PartitionSpec as P


def layer_norm(values):
    center = jnp.mean(values, axis=-1, keepdims=True)
    shifted = values - center
    spread = jnp.mean(shifted * shifted, axis=-1, keepdims=True)
    return shifted * lax.rsqrt(spread + 1e-05)


def add_rows(normed, piece):
    return jnp.dot(normed, piece, preferred_element_type=jnp.float32)


def retention(queries, keys_scaled, values_all, gates_all, start_state, counts_int, head_ids):
    row_count = queries.shape[0]
    draft_len = queries.shape[1]
    heads_dev = start_state.shape[1]
    key_dim = start_state.shape[2]
    value_dim = start_state.shape[3]
    query_heads = queries.reshape(row_count, draft_len, heads_dev, key_dim)
    key_heads = keys_scaled.reshape(row_count, draft_len, heads_dev, key_dim)
    value_heads = values_all.reshape(row_count, draft_len, heads_dev, value_dim)
    gate_heads = gates_all.reshape(row_count, draft_len, heads_dev, value_dim)
    decay_rate = 1.0 - jnp.exp2(-5.0 - head_ids)
    positions = jnp.arange(draft_len, dtype=jnp.float32)
    distance = positions[:, None] - positions[None, :]
    causal = distance >= 0.0
    decay_mask = jnp.where(
        causal[None], jnp.power(decay_rate[:, None, None], jnp.maximum(distance, 0.0)[None]), 0.0
    )
    scores = (
        jnp.einsum("nthk,nshk->nhts", query_heads, key_heads, preferred_element_type=jnp.float32)
        * decay_mask[None]
    )
    weights = scores.astype(jnp.bfloat16)
    inside_terms = jnp.einsum(
        "nhts,nshv->nthv", weights, value_heads, preferred_element_type=jnp.float32
    )
    state_terms = jnp.einsum(
        "nthk,nhkv->nthv", query_heads, start_state, preferred_element_type=jnp.float32
    )
    state_terms = (
        state_terms * jnp.power(decay_rate[None, :], positions[:, None] + 1.0)[None, :, :, None]
    )
    mixture = layer_norm(inside_terms + state_terms)
    hidden = (jax.nn.silu(gate_heads.astype(jnp.float32)) * mixture).astype(jnp.bfloat16)
    hidden = hidden.reshape(row_count, draft_len, heads_dev * value_dim)
    counts = counts_int.astype(jnp.float32)[:, None]
    remaining = jnp.maximum(counts - 1.0 - positions[None, :], 0.0)
    within = positions[None, :] < counts
    scale_rows = jnp.where(
        within[:, :, None], jnp.power(decay_rate[None, None, :], remaining[:, :, None]), 0.0
    )
    kept_keys = (key_heads.astype(jnp.float32) * scale_rows[..., None]).astype(jnp.bfloat16)
    updated = jnp.einsum(
        "nshk,nshv->nhkv", kept_keys, value_heads, preferred_element_type=jnp.float32
    )
    updated = updated + jnp.power(decay_rate[None, :], counts)[
        :, :, None, None
    ] * start_state.astype(jnp.float32)
    return (hidden, updated.astype(jnp.bfloat16))


def per_device(
    draft_ids, worker_slot, accepted, embedding, w_query, w_key, w_value, w_gate, old_state
):
    own_rows = worker_slot.shape[0]
    width_req = lax.axis_size("req")
    my_index = lax.axis_index("req")
    all_ids, all_slots, all_counts = (
        lax.all_gather(draft_ids, "req", axis=0, tiled=True),
        lax.all_gather(worker_slot, "req", axis=0, tiled=True),
        lax.all_gather(accepted, "req", axis=0, tiled=True),
    )
    total_rows = all_slots.shape[0]
    holder = (
        jnp.zeros((total_rows,), jnp.int32)
        .at[all_slots]
        .set(jnp.arange(total_rows, dtype=jnp.int32))
    )
    vocab_rows = embedding.shape[0]
    local_ids = all_ids - my_index * vocab_rows
    inside = (local_ids >= 0) & (local_ids < vocab_rows)
    looked = jnp.take(embedding, jnp.clip(local_ids, 0, vocab_rows - 1), axis=0)
    partial_rows = jnp.where(inside[:, :, None], looked.astype(jnp.float32), 0.0)
    token_cols = lax.psum_scatter(
        partial_rows.astype(jnp.bfloat16), "req", scatter_dimension=0, tiled=True
    )
    tokens = lax.all_gather(token_cols, "head", axis=2, tiled=True)
    draft_len = tokens.shape[1]
    normed = (
        layer_norm(tokens.astype(jnp.float32))
        .astype(jnp.bfloat16)
        .reshape(own_rows * draft_len, tokens.shape[2])
    )

    def add_one(piece):
        return add_rows(normed, piece)

    raw_query = add_one(lax.all_gather(w_query, "req", axis=0, tiled=True))
    raw_key = add_one(lax.all_gather(w_key, "req", axis=0, tiled=True))
    raw_value = add_one(lax.all_gather(w_value, "req", axis=0, tiled=True))
    raw_gate = add_one(lax.all_gather(w_gate, "req", axis=0, tiled=True))
    key_scale = old_state.shape[2] ** (-0.5)
    queries = raw_query.astype(jnp.bfloat16).reshape(own_rows, draft_len, -1)
    keys_scaled = (raw_key * key_scale).astype(jnp.bfloat16).reshape(own_rows, draft_len, -1)
    values_all = raw_value.astype(jnp.bfloat16).reshape(own_rows, draft_len, -1)
    gates_all = raw_gate.astype(jnp.bfloat16).reshape(own_rows, draft_len, -1)
    heads_dev = old_state.shape[1]
    head_ids = (lax.axis_index("head") * heads_dev + jnp.arange(heads_dev, dtype=jnp.int32)).astype(
        jnp.float32
    )
    my_requests = lax.dynamic_slice_in_dim(holder, my_index * own_rows, own_rows)
    source = my_requests // own_rows
    target = worker_slot // own_rows
    to_worker = (
        jnp.zeros((width_req,), jnp.int32).at[target].set(jnp.arange(own_rows, dtype=jnp.int32))
    )
    answer, new_state = retention(
        queries, keys_scaled, values_all, gates_all, old_state, accepted, head_ids
    )
    received = lax.all_to_all(
        jnp.take(answer, to_worker, axis=0), "req", split_axis=0, concat_axis=0, tiled=True
    )
    hidden = jnp.take(received, source, axis=0)
    return (hidden, new_state)


def solution(mesh):
    return jax.shard_map(
        per_device,
        mesh=mesh,
        in_specs=(
            P("req", None),
            P("req"),
            P("req"),
            P("req", "head"),
            P("req", "head"),
            P("req", "head"),
            P("req", "head"),
            P("req", "head"),
            P("req", "head", None, None),
        ),
        out_specs=(P("req", None, "head"), P("req", "head", None, None)),
        check_vma=False,
    )
```

profile of v0, /device:TPU:11, one launch (start us, length us, event | category | flops | bytes accessed | tf_op | source)
XLA Modules:
  0.0 497.8 jit_solution(5932785029727653407)
XLA Ops:
  7.2 16.2 %all_gather.21 = s32[256,16]{1,0:T(8,128)S(1)} all-gather(s32[16,16]{1,0:T(8,128)} %param.11), channel_id=1, replica_groups=mesh['req'=16,'head'=2] {'req'}, dimensions={0}, use_global_device_ids=true | all-gather | bytes 17408 | tf_op jit(solution)/shard_map/all_gather | solution.py:75
  23.5 0.1 copy.43
  23.6 0.1 reshape.228
  23.8 0.1 copy.42
  23.9 0.1 copy.41
  24.0 25.2 %gather_fusion = bf16[4096,1024]{1,0:T(8,128)(2,1)} fusion(bf16[4000,1024]{1,0:T(8,128)(2,1)} %param.14, s32[4096]{0:T(1024)S(1)} %broadcast_clamp_fusion), kind=kCustom, calls=%fused_computation.2 | custom fusion | bytes 16793600 | tf_op jit(solution)/shard_map/jit(_take)/gather | solution.py:88
  49.2 7.9 %select_convert_fusion = bf16[256,16,1024]{2,1,0:T(8,128)(2,1)} fusion(bf16[256,16,1024]{2,1,0:T(8,128)(2,1)} %bitcast.21, pred[256,16]{1,0:T(8,128)(4,1)S(1)} %copy.42, pred[256,16]{1,0:T(8,128)(4,1)S(1)} %copy.41), kind=kLoop, calls=%fused_computation.6 | loop fusion | flops 16777216 | bytes 16785408 | tf_op jit(solution)/shard_map/convert_element_type | solution.py:91
  57.2 107.9 %reduce-scatter.2.cloned.1.call-done = bf16[16,16,1024]{2,1,0:T(8,128)(2,1)} async-done(((bf16[256,16,1024]{2,1,0:T(8,128)(2,1)}), bf16[16,16,1024]{2,1,0:T(8,128)(2,1)}) %reduce-scatter.2.cloned.1.call-update) | async-done | bytes 524304 | tf_op jit(solution)/shard_map/reduce_scatter | solution.py:90
  165.2 0.7 all-gather.12.cloned.1.call-update
  165.9 0.5 all-gather.14.cloned.1.call-update
  166.5 0.5 all-gather.10.cloned.1.call-update
  167.1 0.5 all-gather.8.cloned.1.call-update
  167.9 0.6 scatter_custom_fusion
  168.5 0.6 dynamic-slice
  169.8 0.2 dynamic-update-slice
  170.0 7.4 %all-reduce = s32[256]{0:T(256)S(1)} all-reduce(s32[256]{0:T(256)S(1)} %dynamic-update-slice), channel_id=1, replica_groups=mesh['req'=16,'head'=2] {'req'}, use_global_device_ids=true, to_apply=%add | all-reduce | flops 256 | bytes 2048
  177.4 1.4 scatter_custom_fusion.1
  178.8 0.1 compare_and_fusion.2
  179.1 0.1 power_select_fusion.1
  179.2 8.5 %all-gather.6.cloned.1.call-done = bf16[16,16,2048]{2,1,0:T(8,128)(2,1)} async-done(((bf16[16,16,1024]{2,1,0:T(8,128)(2,1)}), bf16[16,16,2048]{2,1,0:T(8,128)(2,1)}) %all-gather.6.cloned.1.call-update) | async-done | bytes 1048592 | tf_op jit(solution)/shard_map/all_gather | solution.py:93
  187.7 1.4 convert_reduce_fusion
  189.2 1.6 fusion.3
  190.8 1.6 fusion.4
  192.4 47.8 %all-gather.12.cloned.1.call-done = bf16[2048,1024]{1,0:T(8,128)(2,1)} async-done(((bf16[128,1024]{1,0:T(8,128)(2,1)}), bf16[2048,1024]{1,0:T(8,128)(2,1)}) %all-gather.12.cloned.1.call-update) | async-done | bytes 4194320 | tf_op jit(solution)/shard_map/all_gather | solution.py:104
  240.2 3.4 convolution_convert_fusion.2
  243.6 0.4 reshape_reshape.11
  244.0 47.3 %all-gather.14.cloned.1.call-done = bf16[2048,1024]{1,0:T(8,128)(2,1)} async-done(((bf16[128,1024]{1,0:T(8,128)(2,1)}), bf16[2048,1024]{1,0:T(8,128)(2,1)}) %all-gather.14.cloned.1.call-update) | async-done | bytes 4194320 | tf_op jit(solution)/shard_map/all_gather | solution.py:105
  291.3 3.4 fusion.6
  294.7 1.2 reshape_reshape.12
  295.9 9.8 %fusion.15 = f32[16,4,16,512]{3,2,1,0:T(8,128)} fusion(bf16[16,4,256,512]{3,2,1,0:T(8,128)(2,1)} %param.19, bf16[16,16,4,256]{3,2,1,0:T(4,128)(2,1)S(1)} %reshape_reshape.11), kind=kOutput, calls=%fused_computation.34 | convolution fusion | flops 268435456 | bytes 19398656 | tf_op jit(solution)/shard_map/nthk,nhkv->nthv/dot_general | solution.py:43
  305.7 60.4 %all-gather.10.cloned.1.call-done = bf16[2048,2048]{1,0:T(8,128)(2,1)} async-done(((bf16[128,2048]{1,0:T(8,128)(2,1)}), bf16[2048,2048]{1,0:T(8,128)(2,1)}) %all-gather.10.cloned.1.call-update) | async-done | bytes 8388624 | tf_op jit(solution)/shard_map/all_gather | solution.py:106
  366.1 6.7 %convolution_convert_fusion = bf16[256,2048]{1,0:T(8,128)(2,1)} fusion(bf16[256,2048]{1,0:T(8,128)(2,1)S(1)} %bitcast.25, bf16[2048,2048]{1,0:T(8,128)(2,1)} %all-gather.10.cloned.1.call-done), kind=kOutput, calls=%fused_computation.9 | convolution fusion | flops 2148007936 | bytes 10485760 | tf_op jit(solution)/shard_map/dot_general | solution.py:15
  372.8 1.8 reshape_reshape.10
  374.6 2.9 fusion.26
  377.6 0.5 multiply_reduce_fusion
  378.1 63.2 %all-gather.8.cloned.1.call-done = bf16[2048,2048]{1,0:T(8,128)(2,1)} async-done(((bf16[128,2048]{1,0:T(8,128)(2,1)}), bf16[2048,2048]{1,0:T(8,128)(2,1)}) %all-gather.8.cloned.1.call-update) | async-done | bytes 8388624 | tf_op jit(solution)/shard_map/all_gather | solution.py:107
  441.3 7.4 %fusion = f32[256,2048]{1,0:T(8,128)} fusion(bf16[256,2048]{1,0:T(8,128)(2,1)} %bitcast.26, bf16[2048,2048]{1,0:T(8,128)(2,1)} %all-gather.8.cloned.1.call-done), kind=kOutput, calls=%fused_computation.11 | convolution fusion | flops 2148532224 | bytes 11534336 | tf_op jit(solution)/shard_map/dot_general | solution.py:15
  448.7 3.7 reshape.209
  452.3 2.5 fusion.8
  454.8 1.1 copy.54
  455.9 1.8 gather_fusion.1
  457.8 1.1 broadcast_select_fusion.1
  458.9 5.4 %all-to-all-start = ((bf16[16,16,2048]{2,1,0:T(8,128)(2,1)}), bf16[16,16,2048]{2,1,0:T(8,128)(2,1)S(1)}, u32[]{:S(2)}, u32[]{:S(2)}) async-start(bf16[16,16,2048]{2,1,0:T(8,128)(2,1)} %broadcast_select_fusion.1), calls=%async_computation.1 | async-start | bytes 2097152 | tf_op jit(solution)/shard_map/all_to_all | solution.py:126
  464.4 0.2 power_select_fusion
  464.6 19.5 %add_convert_fusion = bf16[16,4,256,512]{3,2,1,0:T(8,128)(2,1)} fusion(bf16[16,4,256,512]{3,2,1,0:T(8,128)(2,1)} %param.19, f32[16,4]{1,0:T(8,128)S(1)} %copy.53, bf16[16,16,4,512]{3,2,1,0:T(4,128)(2,1)S(1)} %reshape_reshape.10, f32[16,16,4]{1,2,0:T(4,128)S(1)} %power_select_fusion, bf16[16,16,4,256]{3,2,1,0:T(4,128)(2,1)S(1)} %copy-done.1), kind=kOutput, calls=%fused_computation.5 | convolution fusion | flops 302776320 | bytes 35131648 | tf_op jit(solution)/shard_map/nshk,nshv->nhkv/dot_general | solution.py:59
  484.1 5.2 %all-to-all-done = bf16[16,16,2048]{2,1,0:T(8,128)(2,1)S(1)} async-done(((bf16[16,16,2048]{2,1,0:T(8,128)(2,1)}), bf16[16,16,2048]{2,1,0:T(8,128)(2,1)S(1)}, u32[]{:S(2)}, u32[]{:S(2)}) %all-to-all-start) | async-done | bytes 1048608 | tf_op jit(solution)/shard_map/all_to_all | solution.py:126
  489.2 0.6 gather_fusion.2
  489.8 1.1 broadcast_select_fusion
  (46 shorter events, 0.8 us)
Async XLA Ops:
  7.2 158.0 %reduce-scatter.2.cloned.1.call-start = ((), (), s32[]{:S(2)}) async-start(), calls=%async_computation.2 | async-start | bytes 8912896 | tf_op jit(solution)/shard_map/reduce_scatter | solution.py:90
  57.1 110.5 %copy-start.4 = (s32[16]{0:T(128)S(1)}, s32[16]{0:T(128)}, u32[]{:S(2)}) copy-start(s32[16]{0:T(128)} %param.13) | copy-start | bytes 196
  57.1 110.8 %copy-start.3 = (s32[16]{0:T(128)S(1)}, s32[16]{0:T(128)}, u32[]{:S(2)}) copy-start(s32[16]{0:T(128)} %param.12) | copy-start | bytes 196
  57.1 111.4 %copy-start.5 = (u32[32]{0:T(128)S(1)}, u32[32]{0:T(128)}, u32[]{:S(2)}) copy-start(u32[32]{0:T(128)} %constant.98) | copy-start | bytes 388
  57.1 130.6 %all-gather.6.cloned.1.call-start = ((), (), s32[]{:S(2)}) async-start(), calls=%async_computation.3 | async-start | bytes 1572864 | tf_op jit(solution)/shard_map/all_gather | solution.py:93
  165.2 75.0 %all-gather.12.cloned.1.call-start = ((), (), s32[]{:S(2)}) async-start(), calls=%async_computation.6 | async-start | bytes 4456448 | tf_op jit(solution)/shard_map/all_gather | solution.py:104
  165.9 125.4 %all-gather.14.cloned.1.call-start = ((), (), s32[]{:S(2)}) async-start(), calls=%async_computation.7 | async-start | bytes 4456448 | tf_op jit(solution)/shard_map/all_gather | solution.py:105
  166.5 199.6 %all-gather.10.cloned.1.call-start = ((), (), s32[]{:S(2)}) async-start(), calls=%async_computation.5 | async-start | bytes 8912896 | tf_op jit(solution)/shard_map/all_gather | solution.py:106
  167.0 274.2 %all-gather.8.cloned.1.call-start = ((), (), s32[]{:S(2)}) async-start(), calls=%async_computation.4 | async-start | bytes 8912896 | tf_op jit(solution)/shard_map/all_gather | solution.py:107
  192.4 173.7 %copy-start.2 = (bf16[16,16,2048]{2,1,0:T(8,128)(2,1)}, bf16[16,16,2048]{2,1,0:T(8,128)(2,1)S(1)}, u32[]{:S(2)}) copy-start(bf16[16,16,2048]{2,1,0:T(8,128)(2,1)S(1)} %fusion.4) | copy-start | bytes 3145732
  244.0 51.9 %copy-start = (bf16[16,16,4,256]{3,2,1,0:T(4,128)(2,1)}, bf16[16,16,4,256]{3,2,1,0:T(4,128)(2,1)S(1)}, u32[]{:S(2)}) copy-start(bf16[16,16,4,256]{3,2,1,0:T(4,128)(2,1)S(1)} %reshape_reshape.11) | copy-start | bytes 1572868
  454.8 9.7 %copy-start.1 = (bf16[16,16,4,256]{3,2,1,0:T(4,128)(2,1)S(1)}, bf16[16,16,4,256]{3,2,1,0:T(4,128)(2,1)}, u32[]{:S(2)}) copy-start(bf16[16,16,4,256]{3,2,1,0:T(4,128)(2,1)} %reshape_reshape.12) | copy-start | bytes 1572868
  458.9 30.3 %all-to-all-start = ((bf16[16,16,2048]{2,1,0:T(8,128)(2,1)}), bf16[16,16,2048]{2,1,0:T(8,128)(2,1)S(1)}, u32[]{:S(2)}, u32[]{:S(2)}) async-start(bf16[16,16,2048]{2,1,0:T(8,128)(2,1)} %broadcast_select_fusion.1), calls=%async_computation.1 | async-start | bytes 2097152 | tf_op jit(solution)/shard_map/all_to_all | solution.py:126
Sparse Core Ops, SparseCore 0:
  57.3 107.8 reduce-scatter.1
  166.7 21.0 all-gather.5
  189.9 50.2 all-gather.11
  242.2 49.0 all-gather.13
  293.3 72.7 all-gather.9
  368.1 73.1 all-gather.7
where the time goes:
time: 499 us; the launch traced here: 498 us
  waiting for transfers between devices  343 us (69%)
  matrix products  53 us (11%)
  local copies, waits for them, and re-layouts  39.3 us (8%)
  blocking collectives  23.6 us (5%)
  other arithmetic  18.4 us (4%)
  between operations  15.1 us (3%)
  starting transfers between devices  5.64 us (1%)
    reduce_scatter x1, waiting for transfers between devices, per_device(): lax.psum_scatter(partial_rows.astype(jnp.bfloat16), 'req', scatter_dimens...  108 us
    all_gather x1, waiting for transfers between devices, per_device(): raw_gate = add_one(lax.all_gather(w_gate, 'req', axis=0, tiled=True))  63.2 us
    all_gather x1, waiting for transfers between devices, per_device(): raw_value = add_one(lax.all_gather(w_value, 'req', axis=0, tiled=True))  60.4 us
    all_gather x1, waiting for transfers between devices, per_device(): raw_query = add_one(lax.all_gather(w_query, 'req', axis=0, tiled=True))  47.8 us
    all_gather x1, waiting for transfers between devices, per_device(): raw_key = add_one(lax.all_gather(w_key, 'req', axis=0, tiled=True))  47.3 us
    gather x1, local copies, waits for them, and re-layouts, per_device(): looked = jnp.take(embedding, jnp.clip(local_ids, 0, vocab_rows - 1), axis=0)  25.2 us
    dot_general x4, matrix products, add_rows(): return jnp.dot(normed, piece, preferred_element_type=jnp.float32)  20.9 us
    dot_general x1, matrix products, retention(): jnp.einsum('nshk,nshv->nhkv', kept_keys, value_heads, preferred_element_t...  19.5 us
  transfers between devices with their start and end apart: 7, of which 7 were waited for; matrix products, arithmetic and copies ran while one was open for 12% of the time, Pallas kernels for 0%

commit v1 on v0

--- a/solution.py
+++ b/solution.py
@@ -123,9 +123,19 @@
     answer, new_state = retention(
         queries, keys_scaled, values_all, gates_all, old_state, accepted, head_ids
     )
-    received = lax.all_to_all(
-        jnp.take(answer, to_worker, axis=0), "req", split_axis=0, concat_axis=0, tiled=True
-    )
+    x = jnp.take(answer, to_worker, axis=0)
+    ways, here = (lax.axis_size("req"), lax.axis_index("req"))
+    width = x.shape[0] // ways
+    lengths = list(x.shape)
+    lengths[0] = width
+    height = lengths[0]
+    lengths[0] = height * ways
+    received = jnp.zeros(lengths, x.dtype)
+    for mask in range(ways):
+        part = lax.dynamic_slice_in_dim(x, (here ^ mask) * width, width, axis=0)
+        if mask:
+            part = lax.ppermute(part, "req", [(d, d ^ mask) for d in range(ways)])
+        received = lax.dynamic_update_slice_in_dim(received, part, (here ^ mask) * height, axis=0)
     hidden = jnp.take(received, source, axis=0)
     return (hidden, new_state)
 

time: 499 us -> 523 us (1.048)
  starting transfers between devices: 5.64 us -> 18.1 us
  waiting for transfers between devices: 343 us -> 349 us
  local copies, waits for them, and re-layouts: 39.3 us -> 44.7 us
    ppermute x0 -> x15, starting transfers between devices: none -> 17.9 us  [per_device(): part = lax.ppermute(part, 'req', [(d, d ^ mask) for d in range(ways)])]
    ppermute x0 -> x15, waiting for transfers between devices: none -> 12.5 us  [per_device(): part = lax.ppermute(part, 'req', [(d, d ^ mask) for d in range(ways)])]
    all_to_all x1 -> x0, starting transfers between devices: 5.41 us -> none  [per_device(): lax.all_to_all(jnp.take(answer, to_worker, axis=0), 'req', split_axis=0,...]
  transfers between devices with their start and end apart: 7 -> 21, of which waited for: 7 -> 10; matrix products, arithmetic and copies ran while one was open for 12% -> 12% of each run, Pallas kernels for 0% -> 0%
where the time goes in v1:
time: 523 us; the launch traced here: 522 us
  waiting for transfers between devices  349 us (67%)
  matrix products  53 us (10%)
  local copies, waits for them, and re-layouts  44.7 us (9%)
  blocking collectives  23.6 us (5%)
  starting transfers between devices  18.1 us (3%)
  other arithmetic  17.5 us (3%)
  between operations  15.3 us (3%)
    reduce_scatter x1, waiting for transfers between devices, per_device(): lax.psum_scatter(partial_rows.astype(jnp.bfloat16), 'req', scatter_dimens...  108 us
    all_gather x1, waiting for transfers between devices, per_device(): raw_gate = add_one(lax.all_gather(w_gate, 'req', axis=0, tiled=True))  63.2 us
    all_gather x1, waiting for transfers between devices, per_device(): raw_value = add_one(lax.all_gather(w_value, 'req', axis=0, tiled=True))  60.4 us
    all_gather x1, waiting for transfers between devices, per_device(): raw_query = add_one(lax.all_gather(w_query, 'req', axis=0, tiled=True))  47.8 us
    all_gather x1, waiting for transfers between devices, per_device(): raw_key = add_one(lax.all_gather(w_key, 'req', axis=0, tiled=True))  47.3 us
    gather x1, local copies, waits for them, and re-layouts, per_device(): looked = jnp.take(embedding, jnp.clip(local_ids, 0, vocab_rows - 1), axis=0)  25.2 us
    dot_general x4, matrix products, add_rows(): return jnp.dot(normed, piece, preferred_element_type=jnp.float32)  20.9 us
    dot_general x1, matrix products, retention(): jnp.einsum('nshk,nshv->nhkv', kept_keys, value_heads, preferred_element_t...  19.5 us
  transfers between devices with their start and end apart: 21, of which 10 were waited for; matrix products, arithmetic and copies ran while one was open for 12% of the time, Pallas kernels for 0%

profile of v1, /device:TPU:11, one launch (start us, length us, event | category | flops | bytes accessed | tf_op | source)
XLA Modules:
  0.0 521.7 jit_solution(17641157134163181821)
XLA Ops:
  7.2 16.2 %all_gather.21 = s32[256,16]{1,0:T(8,128)S(1)} all-gather(s32[16,16]{1,0:T(8,128)} %param.11), channel_id=1, replica_groups=mesh['req'=16,'head'=2] {'req'}, dimensions={0}, use_global_device_ids=true | all-gather | bytes 17408 | tf_op jit(solution)/shard_map/all_gather | solution.py:75
  24.0 25.2 %gather_fusion = bf16[4096,1024]{1,0:T(8,128)(2,1)} fusion(bf16[4000,1024]{1,0:T(8,128)(2,1)} %param.14, s32[4096]{0:T(1024)S(1)} %broadcast_clamp_fusion), kind=kCustom, calls=%fused_computation.2 | custom fusion | bytes 16793600 | tf_op jit(solution)/shard_map/jit(_take)/gather | solution.py:88
  49.2 7.9 %select_convert_fusion = bf16[256,16,1024]{2,1,0:T(8,128)(2,1)} fusion(bf16[256,16,1024]{2,1,0:T(8,128)(2,1)} %bitcast.21, pred[256,16]{1,0:T(8,128)(4,1)S(1)} %copy.42, pred[256,16]{1,0:T(8,128)(4,1)S(1)} %copy.41), kind=kLoop, calls=%fused_computation.6 | loop fusion | flops 16777216 | bytes 16785408 | tf_op jit(solution)/shard_map/convert_element_type | solution.py:91
  57.2 107.9 %reduce-scatter.2.cloned.1.call-done = bf16[16,16,1024]{2,1,0:T(8,128)(2,1)} async-done(((bf16[256,16,1024]{2,1,0:T(8,128)(2,1)}), bf16[16,16,1024]{2,1,0:T(8,128)(2,1)}) %reduce-scatter.2.cloned.1.call-update) | async-done | bytes 524304 | tf_op jit(solution)/shard_map/reduce_scatter | solution.py:90
  170.2 7.4 %all-reduce = s32[256]{0:T(256)S(1)} all-reduce(s32[256]{0:T(256)S(1)} %dynamic-update-slice), channel_id=1, replica_groups=mesh['req'=16,'head'=2] {'req'}, use_global_device_ids=true, to_apply=%add | all-reduce | flops 256 | bytes 2048
  177.6 1.6 scatter_custom_fusion.1
  179.8 7.9 %all-gather.6.cloned.1.call-done = bf16[16,16,2048]{2,1,0:T(8,128)(2,1)} async-done(((bf16[16,16,1024]{2,1,0:T(8,128)(2,1)}), bf16[16,16,2048]{2,1,0:T(8,128)(2,1)}) %all-gather.6.cloned.1.call-update) | async-done | bytes 1048592 | tf_op jit(solution)/shard_map/all_gather | solution.py:93
  187.7 1.4 convert_reduce_fusion
  189.2 1.6 fusion.3
  190.8 1.6 fusion.4
  192.4 47.8 %all-gather.12.cloned.1.call-done = bf16[2048,1024]{1,0:T(8,128)(2,1)} async-done(((bf16[128,1024]{1,0:T(8,128)(2,1)}), bf16[2048,1024]{1,0:T(8,128)(2,1)}) %all-gather.12.cloned.1.call-update) | async-done | bytes 4194320 | tf_op jit(solution)/shard_map/all_gather | solution.py:104
  240.2 3.4 convolution_convert_fusion.2
  244.0 47.3 %all-gather.14.cloned.1.call-done = bf16[2048,1024]{1,0:T(8,128)(2,1)} async-done(((bf16[128,1024]{1,0:T(8,128)(2,1)}), bf16[2048,1024]{1,0:T(8,128)(2,1)}) %all-gather.14.cloned.1.call-update) | async-done | bytes 4194320 | tf_op jit(solution)/shard_map/all_gather | solution.py:105
  291.3 3.4 fusion.6
  294.7 1.2 reshape_reshape.12
  295.9 9.8 %fusion.15 = f32[16,4,16,512]{3,2,1,0:T(8,128)} fusion(bf16[16,4,256,512]{3,2,1,0:T(8,128)(2,1)} %param.19, bf16[16,16,4,256]{3,2,1,0:T(4,128)(2,1)S(1)} %reshape_reshape.11), kind=kOutput, calls=%fused_computation.34 | convolution fusion | flops 268435456 | bytes 19398656 | tf_op jit(solution)/shard_map/nthk,nhkv->nthv/dot_general | solution.py:43
  305.7 60.4 %all-gather.10.cloned.1.call-done = bf16[2048,2048]{1,0:T(8,128)(2,1)} async-done(((bf16[128,2048]{1,0:T(8,128)(2,1)}), bf16[2048,2048]{1,0:T(8,128)(2,1)}) %all-gather.10.cloned.1.call-update) | async-done | bytes 8388624 | tf_op jit(solution)/shard_map/all_gather | solution.py:106
  366.1 6.7 %convolution_convert_fusion = bf16[256,2048]{1,0:T(8,128)(2,1)} fusion(bf16[256,2048]{1,0:T(8,128)(2,1)S(1)} %bitcast.25, bf16[2048,2048]{1,0:T(8,128)(2,1)} %all-gather.10.cloned.1.call-done), kind=kOutput, calls=%fused_computation.9 | convolution fusion | flops 2148007936 | bytes 10485760 | tf_op jit(solution)/shard_map/dot_general | solution.py:15
  372.8 1.8 reshape_reshape.10
  374.6 2.9 fusion.26
  378.1 63.2 %all-gather.8.cloned.1.call-done = bf16[2048,2048]{1,0:T(8,128)(2,1)} async-done(((bf16[128,2048]{1,0:T(8,128)(2,1)}), bf16[2048,2048]{1,0:T(8,128)(2,1)}) %all-gather.8.cloned.1.call-update) | async-done | bytes 8388624 | tf_op jit(solution)/shard_map/all_gather | solution.py:107
  441.3 7.4 %fusion = f32[256,2048]{1,0:T(8,128)} fusion(bf16[256,2048]{1,0:T(8,128)(2,1)} %bitcast.26, bf16[2048,2048]{1,0:T(8,128)(2,1)} %all-gather.8.cloned.1.call-done), kind=kOutput, calls=%fused_computation.11 | convolution fusion | flops 2148532224 | bytes 11534336 | tf_op jit(solution)/shard_map/dot_general | solution.py:15
  448.7 3.6 reshape.209
  452.3 2.5 fusion.8
  454.8 1.1 copy.54
  455.9 1.9 gather_fusion.1
  459.1 1.2 collective-permute-start.1
  461.0 0.9 collective-permute-start.3
  462.6 19.5 %add_convert_fusion = bf16[16,4,256,512]{3,2,1,0:T(8,128)(2,1)} fusion(bf16[16,4,256,512]{3,2,1,0:T(8,128)(2,1)} %param.19, f32[16,4]{1,0:T(8,128)S(1)} %copy.53, bf16[16,16,4,512]{3,2,1,0:T(4,128)(2,1)S(1)} %reshape_reshape.10, f32[16,16,4]{1,2,0:T(4,128)S(1)} %power_select_fusion, bf16[16,16,4,256]{3,2,1,0:T(4,128)(2,1)S(1)} %copy-done.1), kind=kOutput, calls=%fused_computation.5 | convolution fusion | flops 302776320 | bytes 35131648 | tf_op jit(solution)/shard_map/nshk,nshv->nhkv/dot_general | solution.py:59
  482.1 1.8 collective-permute-start.5
  483.8 0.8 constant_dynamic-update-slice_fusion.14
  484.7 1.1 collective-permute-start.6
  485.8 0.8 constant_dynamic-update-slice_fusion.13
  486.6 1.1 collective-permute-start.7
  487.7 0.8 constant_dynamic-update-slice_fusion.12
  488.6 1.5 collective-permute-start.8
  490.1 0.8 constant_dynamic-update-slice_fusion.11
  490.9 1.9 collective-permute-start.9
  492.9 0.8 constant_dynamic-update-slice_fusion.10
  493.7 1.9 collective-permute-start.10
  495.6 1.0 collective-permute-start.11
  497.4 1.9 collective-permute-start.13
  499.3 1.2 collective-permute-start.14
  500.6 6.6 %collective-permute-done.11 = bf16[1,16,2048]{2,1,0:T(8,128)(2,1)S(1)} collective-permute-done((bf16[1,16,2048]{2,1,0:T(8,128)(2,1)S(1)}, bf16[1,16,2048]{2,1,0:T(8,128)(2,1)S(1)}, u32[]{:S(2)}, u32[]{:S(2)}) %collective-permute-start.11) | collective-permute-done | bytes 65568 | tf_op jit(solution)/shard_map/ppermute | solution.py:137
  507.2 2.5 collective-permute-done.12
  509.7 1.9 collective-permute-done.13
  511.6 1.4 collective-permute-done.14
  513.7 1.1 broadcast_select_fusion
  (91 shorter events, 10.4 us)
Async XLA Ops:
  7.2 158.0 %reduce-scatter.2.cloned.1.call-start = ((), (), s32[]{:S(2)}) async-start(), calls=%async_computation.1 | async-start | bytes 8912896 | tf_op jit(solution)/shard_map/reduce_scatter | solution.py:90
  57.1 110.6 %copy-start.4 = (s32[16]{0:T(128)S(1)}, s32[16]{0:T(128)}, u32[]{:S(2)}) copy-start(s32[16]{0:T(128)} %param.13) | copy-start | bytes 196
  57.1 110.8 %copy-start.3 = (s32[16]{0:T(128)S(1)}, s32[16]{0:T(128)}, u32[]{:S(2)}) copy-start(s32[16]{0:T(128)} %param.12) | copy-start | bytes 196
  57.1 111.6 %copy-start.5 = (u32[32]{0:T(128)S(1)}, u32[32]{0:T(128)}, u32[]{:S(2)}) copy-start(u32[32]{0:T(128)} %constant.126) | copy-start | bytes 388
  57.1 130.6 %all-gather.6.cloned.1.call-start = ((), (), s32[]{:S(2)}) async-start(), calls=%async_computation.2 | async-start | bytes 1572864 | tf_op jit(solution)/shard_map/all_gather | solution.py:93
  165.2 75.0 %all-gather.12.cloned.1.call-start = ((), (), s32[]{:S(2)}) async-start(), calls=%async_computation.5 | async-start | bytes 4456448 | tf_op jit(solution)/shard_map/all_gather | solution.py:104
  165.9 125.4 %all-gather.14.cloned.1.call-start = ((), (), s32[]{:S(2)}) async-start(), calls=%async_computation.6 | async-start | bytes 4456448 | tf_op jit(solution)/shard_map/all_gather | solution.py:105
  166.5 199.6 %all-gather.10.cloned.1.call-start = ((), (), s32[]{:S(2)}) async-start(), calls=%async_computation.4 | async-start | bytes 8912896 | tf_op jit(solution)/shard_map/all_gather | solution.py:106
  167.1 274.2 %all-gather.8.cloned.1.call-start = ((), (), s32[]{:S(2)}) async-start(), calls=%async_computation.3 | async-start | bytes 8912896 | tf_op jit(solution)/shard_map/all_gather | solution.py:107
  192.4 173.7 %copy-start.2 = (bf16[16,16,2048]{2,1,0:T(8,128)(2,1)}, bf16[16,16,2048]{2,1,0:T(8,128)(2,1)S(1)}, u32[]{:S(2)}) copy-start(bf16[16,16,2048]{2,1,0:T(8,128)(2,1)S(1)} %fusion.4) | copy-start | bytes 3145732
  244.0 51.9 %copy-start = (bf16[16,16,4,256]{3,2,1,0:T(4,128)(2,1)}, bf16[16,16,4,256]{3,2,1,0:T(4,128)(2,1)S(1)}, u32[]{:S(2)}) copy-start(bf16[16,16,4,256]{3,2,1,0:T(4,128)(2,1)S(1)} %reshape_reshape.11) | copy-start | bytes 1572868
  455.9 6.7 %copy-start.1 = (bf16[16,16,4,256]{3,2,1,0:T(4,128)(2,1)S(1)}, bf16[16,16,4,256]{3,2,1,0:T(4,128)(2,1)}, u32[]{:S(2)}) copy-start(bf16[16,16,4,256]{3,2,1,0:T(4,128)(2,1)} %reshape_reshape.12) | copy-start | bytes 1572868
  458.9 23.2 %collective-permute-start = (bf16[1,16,2048]{2,1,0:T(8,128)(2,1)}, bf16[1,16,2048]{2,1,0:T(8,128)(2,1)}, u32[]{:S(2)}, u32[]{:S(2)}) collective-permute-start(bf16[1,16,2048]{2,1,0:T(8,128)(2,1)} %get-tuple-element.21), channel_id=1, source_target_pairs={{0,2},{2,0},{4,6},{6,4},{8,10},{10,8},{12,14},{14,12},{16,18},{18,... | collective-permute-start | bytes 196616 | tf_op jit(solution)/shard_map/ppermute | solution.py:137
  459.1 25.6 %collective-permute-start.1 = (bf16[1,16,2048]{2,1,0:T(8,128)(2,1)}, bf16[1,16,2048]{2,1,0:T(8,128)(2,1)}, u32[]{:S(2)}, u32[]{:S(2)}) collective-permute-start(bf16[1,16,2048]{2,1,0:T(8,128)(2,1)} %get-tuple-element.20), channel_id=1, source_target_pairs={{0,4},{2,6},{4,0},{6,2},{8,12},{10,14},{12,8},{14,10},{16,20},{18,... | collective-permute-start | bytes 196616 | tf_op jit(solution)/shard_map/ppermute | solution.py:137
  460.3 26.3 %collective-permute-start.2 = (bf16[1,16,2048]{2,1,0:T(8,128)(2,1)S(1)}, bf16[1,16,2048]{2,1,0:T(8,128)(2,1)}, u32[]{:S(2)}, u32[]{:S(2)}) collective-permute-start(bf16[1,16,2048]{2,1,0:T(8,128)(2,1)S(1)} %get-tuple-element.19), channel_id=1, source_target_pairs={{0,6},{2,4},{4,2},{6,0},{8,14},{10,12},{12,10},{14,8},{16,22},{18,... | collective-permute-start | bytes 196616 | tf_op jit(solution)/shard_map/ppermute | solution.py:137
  461.0 27.6 %collective-permute-start.3 = (bf16[1,16,2048]{2,1,0:T(8,128)(2,1)S(1)}, bf16[1,16,2048]{2,1,0:T(8,128)(2,1)}, u32[]{:S(2)}, u32[]{:S(2)}) collective-permute-start(bf16[1,16,2048]{2,1,0:T(8,128)(2,1)S(1)} %get-tuple-element.18), channel_id=1, source_target_pairs={{0,8},{2,10},{4,12},{6,14},{8,0},{10,2},{12,4},{14,6},{16,24},{18,... | collective-permute-start | bytes 196616 | tf_op jit(solution)/shard_map/ppermute | solution.py:137
  461.9 29.1 %collective-permute-start.4 = (bf16[1,16,2048]{2,1,0:T(8,128)(2,1)S(1)}, bf16[1,16,2048]{2,1,0:T(8,128)(2,1)}, u32[]{:S(2)}, u32[]{:S(2)}) collective-permute-start(bf16[1,16,2048]{2,1,0:T(8,128)(2,1)S(1)} %get-tuple-element.17), channel_id=1, source_target_pairs={{0,10},{2,8},{4,14},{6,12},{8,2},{10,0},{12,6},{14,4},{16,26},{18,... | collective-permute-start | bytes 196616 | tf_op jit(solution)/shard_map/ppermute | solution.py:137
  482.1 11.6 %collective-permute-start.5 = (bf16[1,16,2048]{2,1,0:T(8,128)(2,1)S(1)}, bf16[1,16,2048]{2,1,0:T(8,128)(2,1)S(1)}, u32[]{:S(2)}, u32[]{:S(2)}) collective-permute-start(bf16[1,16,2048]{2,1,0:T(8,128)(2,1)S(1)} %get-tuple-element.16), channel_id=1, source_target_pairs={{0,12},{2,14},{4,8},{6,10},{8,4},{10,6},{12,0},{14,2},{16,28},{18,... | collective-permute-start | bytes 196616 | tf_op jit(solution)/shard_map/ppermute | solution.py:137
  484.7 10.9 %collective-permute-start.6 = (bf16[1,16,2048]{2,1,0:T(8,128)(2,1)S(1)}, bf16[1,16,2048]{2,1,0:T(8,128)(2,1)S(1)}, u32[]{:S(2)}, u32[]{:S(2)}) collective-permute-start(bf16[1,16,2048]{2,1,0:T(8,128)(2,1)S(1)} %get-tuple-element.15), channel_id=1, source_target_pairs={{0,14},{2,12},{4,10},{6,8},{8,6},{10,4},{12,2},{14,0},{16,30},{18,... | collective-permute-start | bytes 196616 | tf_op jit(solution)/shard_map/ppermute | solution.py:137
  486.6 10.1 %collective-permute-start.7 = (bf16[1,16,2048]{2,1,0:T(8,128)(2,1)S(1)}, bf16[1,16,2048]{2,1,0:T(8,128)(2,1)S(1)}, u32[]{:S(2)}, u32[]{:S(2)}) collective-permute-start(bf16[1,16,2048]{2,1,0:T(8,128)(2,1)S(1)} %get-tuple-element.14), channel_id=1, source_target_pairs={{0,16},{2,18},{4,20},{6,22},{8,24},{10,26},{12,28},{14,30},{16,0},... | collective-permute-start | bytes 196616 | tf_op jit(solution)/shard_map/ppermute | solution.py:137
  488.6 8.8 %collective-permute-start.8 = (bf16[1,16,2048]{2,1,0:T(8,128)(2,1)S(1)}, bf16[1,16,2048]{2,1,0:T(8,128)(2,1)S(1)}, u32[]{:S(2)}, u32[]{:S(2)}) collective-permute-start(bf16[1,16,2048]{2,1,0:T(8,128)(2,1)S(1)} %get-tuple-element.13), channel_id=1, source_target_pairs={{0,18},{2,16},{4,22},{6,20},{8,26},{10,24},{12,30},{14,28},{16,2},... | collective-permute-start | bytes 196616 | tf_op jit(solution)/shard_map/ppermute | solution.py:137
  490.9 8.4 %collective-permute-start.9 = (bf16[1,16,2048]{2,1,0:T(8,128)(2,1)S(1)}, bf16[1,16,2048]{2,1,0:T(8,128)(2,1)S(1)}, u32[]{:S(2)}, u32[]{:S(2)}) collective-permute-start(bf16[1,16,2048]{2,1,0:T(8,128)(2,1)S(1)} %get-tuple-element.12), channel_id=1, source_target_pairs={{0,20},{2,22},{4,16},{6,18},{8,28},{10,30},{12,24},{14,26},{16,4},... | collective-permute-start | bytes 196616 | tf_op jit(solution)/shard_map/ppermute | solution.py:137
  493.7 6.8 %collective-permute-start.10 = (bf16[1,16,2048]{2,1,0:T(8,128)(2,1)S(1)}, bf16[1,16,2048]{2,1,0:T(8,128)(2,1)S(1)}, u32[]{:S(2)}, u32[]{:S(2)}) collective-permute-start(bf16[1,16,2048]{2,1,0:T(8,128)(2,1)S(1)} %get-tuple-element.11), channel_id=1, source_target_pairs={{0,22},{2,20},{4,18},{6,16},{8,30},{10,28},{12,26},{14,24},{16,6},... | collective-permute-start | bytes 196616 | tf_op jit(solution)/shard_map/ppermute | solution.py:137
  495.6 11.6 %collective-permute-start.11 = (bf16[1,16,2048]{2,1,0:T(8,128)(2,1)S(1)}, bf16[1,16,2048]{2,1,0:T(8,128)(2,1)S(1)}, u32[]{:S(2)}, u32[]{:S(2)}) collective-permute-start(bf16[1,16,2048]{2,1,0:T(8,128)(2,1)S(1)} %get-tuple-element.10), channel_id=1, source_target_pairs={{0,24},{2,26},{4,28},{6,30},{8,16},{10,18},{12,20},{14,22},{16,8},... | collective-permute-start | bytes 196616 | tf_op jit(solution)/shard_map/ppermute | solution.py:137
  496.7 13.0 %collective-permute-start.12 = (bf16[1,16,2048]{2,1,0:T(8,128)(2,1)S(1)}, bf16[1,16,2048]{2,1,0:T(8,128)(2,1)S(1)}, u32[]{:S(2)}, u32[]{:S(2)}) collective-permute-start(bf16[1,16,2048]{2,1,0:T(8,128)(2,1)S(1)} %get-tuple-element.9), channel_id=1, source_target_pairs={{0,26},{2,24},{4,30},{6,28},{8,18},{10,16},{12,22},{14,20},{16,10}... | collective-permute-start | bytes 196616 | tf_op jit(solution)/shard_map/ppermute | solution.py:137
  497.4 14.2 %collective-permute-start.13 = (bf16[1,16,2048]{2,1,0:T(8,128)(2,1)S(1)}, bf16[1,16,2048]{2,1,0:T(8,128)(2,1)S(1)}, u32[]{:S(2)}, u32[]{:S(2)}) collective-permute-start(bf16[1,16,2048]{2,1,0:T(8,128)(2,1)S(1)} %get-tuple-element.8), channel_id=1, source_target_pairs={{0,28},{2,30},{4,24},{6,26},{8,20},{10,22},{12,16},{14,18},{16,12}... | collective-permute-start | bytes 196616 | tf_op jit(solution)/shard_map/ppermute | solution.py:137
  499.3 13.7 %collective-permute-start.14 = (bf16[1,16,2048]{2,1,0:T(8,128)(2,1)S(1)}, bf16[1,16,2048]{2,1,0:T(8,128)(2,1)S(1)}, u32[]{:S(2)}, u32[]{:S(2)}) collective-permute-start(bf16[1,16,2048]{2,1,0:T(8,128)(2,1)S(1)} %get-tuple-element.7), channel_id=1, source_target_pairs={{0,30},{2,28},{4,26},{6,24},{8,22},{10,20},{12,18},{14,16},{16,14}... | collective-permute-start | bytes 196616 | tf_op jit(solution)/shard_map/ppermute | solution.py:137
Sparse Core Ops, SparseCore 0:
  57.3 107.8 reduce-scatter.1
  166.7 21.0 all-gather.5
  189.9 50.2 all-gather.11
  242.2 49.0 all-gather.13
  293.3 72.7 all-gather.9
  368.1 73.1 all-gather.7
